TPU v7x, 1024 devices: a whole 4x8x16 slice. The times are simulated.
1024 devices in a mesh: grp: 128 (over z, y_hi, core), tm: 8 (over x, y_lo).
Axes of the slice: x: 4, y: 8 (y_hi: 4, y_lo: 2; y = y_hi * 2 + y_lo), z: 16, core: 2. Of those that a mesh axis runs over, the one named last changes fastest.
Arguments:
- features: bfloat16 [512, 2048, 1024], P('grp', 'tm'), may hold values from -40 to 40
- frame_counts: int32 [512], P('grp'), may hold values from 512 to 2048
- pool_query: bfloat16 [8, 1024], replicated, may hold values from -4 to 4
- w_proj: bfloat16 [1024, 512], replicated, may hold values from -0.1875 to 0.1875
- doc_embed: bfloat16 [16384, 512], P(('grp', 'tm')), may hold values from -0.25 to 0.25
- doc_index: int32 [512], replicated, may hold values from 0 to 16383
Outputs:
- loss: float32 [512], P('grp')
- speech_grad: float32 [512, 512], P('grp')
- doc_grad: float32 [16384, 512], P(('grp', 'tm'))
All inputs are finite; a program needn't handle non-finite values.
Results may differ from a plain program's by a relative error of at most 0.0044.
Values may be sent and summed in bfloat16 or wider, within the bound.
A program may use at most 32 MiB of HBM per device.

v0:
```python
import math

import jax
import jax.numpy as jnp
from jax import lax
from jax.sharding import PartitionSpec as P

logit_scale = 10.0
logit_shift = -8.0
norm_eps = 1e-06


def passed_along(value, axis, steps):
    count = lax.axis_size(axis)
    pairs = [(source, (source + steps) % count) for source in range(count)]
    return lax.ppermute(value, axis, pairs)


def pair_tile(speech_rows, rec_start, doc_rows, doc_start, doc_index):
    row_count = speech_rows.shape[0]
    logits = (
        logit_scale * jnp.dot(speech_rows, doc_rows.T, preferred_element_type=jnp.float32)
        + logit_shift
    )
    targets = lax.dynamic_slice_in_dim(doc_index, rec_start, row_count)
    doc_ids = doc_start + jnp.arange(doc_rows.shape[0], dtype=jnp.int32)
    labels = jnp.where(targets[:, None] == doc_ids[None, :], 1.0, -1.0)
    losses = jnp.sum(jax.nn.softplus(-labels * logits), axis=1)
    grad_b = (-labels * jax.nn.sigmoid(-labels * logits)).astype(jnp.bfloat16)
    speech_part = logit_scale * jnp.dot(grad_b, doc_rows, preferred_element_type=jnp.float32)
    doc_part = logit_scale * jnp.dot(grad_b.T, speech_rows, preferred_element_type=jnp.float32)
    return (losses, speech_part, doc_part)


def body(features, frame_counts, pool_query, w_proj, doc_embed, doc_index):
    rec_count, frame_dev, channels = features.shape
    width = w_proj.shape[1]
    heads = pool_query.shape[0]
    doc_dev = doc_embed.shape[0]
    values = jnp.dot(
        features.reshape(rec_count * frame_dev, channels),
        w_proj,
        preferred_element_type=jnp.float32,
    ).astype(jnp.bfloat16)
    values = values.reshape(rec_count, frame_dev, heads, width // heads)
    scores = jnp.einsum(
        "rfc,hc->rhf", features, pool_query, preferred_element_type=jnp.float32
    ) / math.sqrt(channels)
    positions = lax.axis_index("tm") * frame_dev + jnp.arange(frame_dev, dtype=jnp.int32)
    valid = (positions[None, :] < frame_counts[:, None])[:, None, :]
    masked = jnp.where(valid, scores, -1e30)
    peak_score = lax.pmax(jnp.max(masked, axis=2), "tm")
    weights = jnp.where(valid, jnp.exp(masked - peak_score[:, :, None]), 0.0)
    totals = jnp.sum(weights, axis=2)
    numerator = jnp.einsum(
        "rhf,rfhd->rhd", weights.astype(jnp.bfloat16), values, preferred_element_type=jnp.float32
    )
    numerator, totals = lax.psum((numerator, totals), "tm")
    pooled = (numerator / totals[:, :, None]).reshape(rec_count, width)
    speech = (
        pooled * lax.rsqrt(jnp.sum(pooled * pooled, axis=1, keepdims=True) + norm_eps)
    ).astype(jnp.bfloat16)
    group = lax.axis_index("grp")
    column = lax.axis_index("tm")
    group_count = lax.axis_size("grp")
    column_count = lax.axis_size("tm")
    loss_zero = jnp.zeros((rec_count,), jnp.float32)
    speech_zero = jnp.zeros((rec_count, width), jnp.float32)
    doc_zero = jnp.zeros((doc_dev, width), jnp.float32)

    def advance_docs(turn, state_tuple):
        blocks, grads, losses, speech_acc = state_tuple
        source = (group - turn) % group_count
        loss_rows, speech_part, doc_part = pair_tile(
            speech, group * rec_count, blocks, (source * column_count + column) * doc_dev, doc_index
        )
        blocks = passed_along(blocks, "grp", 1)
        grads = passed_along(grads + doc_part, "grp", 1)
        return (blocks, grads, losses + loss_rows, speech_acc + speech_part)

    final_state = lax.fori_loop(
        0, group_count, advance_docs, (doc_embed, doc_zero, loss_zero, speech_zero)
    )
    doc_grad = final_state[1]
    loss_part = final_state[2]
    speech_part_sum = final_state[3]
    speech_grad, loss = lax.psum((speech_part_sum, loss_part), "tm")
    return (loss, speech_grad, doc_grad)


def solution(mesh):
    placed = (P("grp", "tm", None), P("grp"), P(), P(), P(("grp", "tm"), None), P())
    return jax.shard_map(
        body,
        mesh=mesh,
        in_specs=placed,
        out_specs=(P("grp"), P("grp", None), P(("grp", "tm"), None)),
        check_vma=False,
    )
```

profile of v0, /device:TPU:256, one launch (start us, length us, event | category | flops | bytes accessed | tf_op | source)
XLA Modules:
  0.0 1641.0 jit_solution(4417146719502107603)
XLA Ops:
  3.7 19.9 %pmax.7 = f32[4,8]{1,0:T(4,128)S(1)} all-reduce(f32[4,8]{1,0:T(4,128)S(1)} %get-tuple-element.294), channel_id=1, replica_groups=mesh['grp'=128,'tm'=8] {'tm'}, use_global_device_ids=true, to_apply=%region_1.2 | all-reduce | flops 32 | bytes 256 | tf_op jit(solution)/shard_map/pmax | solution.py:52
  30.3 30.8 %all-reduce.1 = (f32[4,8,64]{2,1,0:T(8,128)S(1)}, f32[4,8]{1,0:T(4,128)S(1)}) all-reduce(f32[4,8,64]{2,1,0:T(8,128)S(1)} %bitcast.28, f32[4,8]{1,0:T(4,128)S(1)} %get-tuple-element.292), channel_id=1, replica_groups=mesh['grp'=128,'tm'=8] {'tm'}, use_global_device_ids=true, to_apply=%region_2.3 | all-reduce | flops 2080 | bytes 16640 | tf_op jit(solution)/shard_map/psum | solution.py:58
  62.3 1525.1 %while.22 = (s32[]{:T(128)}, bf16[16,512]{1,0:T(8,128)(2,1)S(1)}, f32[16,512]{1,0:T(8,128)S(1)}, f32[4]{0:T(128)S(1)}, f32[4,512]{1,0:T(4,128)S(1)}, /*index=5*/...) while((s32[]{:T(128)}, bf16[16,512]{1,0:T(8,128)(2,1)S(1)}, ...), condition=%wide.region_8.9_spmd.clone, body=%wide.region_6.8_spmd.clone.sunk | while | flops 221030 | bytes 353785 | solution.py:81
  78.8 4.7 collective-permute-done
  90.7 4.7 collective-permute-done
  102.6 4.7 collective-permute-done
  114.5 4.7 collective-permute-done
  138.7 4.7 collective-permute-done
  150.6 4.8 collective-permute-done
  162.5 4.7 collective-permute-done
  186.3 4.7 collective-permute-done
  198.2 4.7 collective-permute-done
  210.1 4.7 collective-permute-done
  222.1 4.7 collective-permute-done
  234.0 4.7 collective-permute-done
  245.9 4.7 collective-permute-done
  257.9 4.8 collective-permute-done
  269.8 4.7 collective-permute-done
  281.7 4.7 collective-permute-done
  293.6 4.7 collective-permute-done
  305.5 4.7 collective-permute-done
  317.4 4.7 collective-permute-done
  341.2 4.7 collective-permute-done
  1587.4 53.0 %all-reduce = (f32[4]{0:T(128)}, f32[4,512]{1,0:T(4,128)}) all-reduce(f32[4]{0:T(128)S(1)} %get-tuple-element.233, f32[4,512]{1,0:T(4,128)S(1)} %get-tuple-element.234), channel_id=1, replica_groups=mesh['grp'=128,'tm'=8] {'tm'}, use_global_device_ids=true, to_apply=%region_9.10 | all-reduce | flops 2052 | bytes 16416 | tf_op jit(solution)/shard_map/psum | solution.py:87
  (1280 shorter events, 1434.6 us)
Async XLA Ops:
  64.7 9.5 collective-permute-start.1
  76.7 9.5 collective-permute-start.1
  88.6 9.5 collective-permute-start.1
  100.5 9.5 collective-permute-start.1
  112.4 9.5 collective-permute-start.1
  124.3 9.8 collective-permute-start.1
  136.5 9.5 collective-permute-start.1
  148.4 9.5 collective-permute-start.1
  160.4 9.5 collective-permute-start.1
  172.3 9.5 collective-permute-start.1
  184.2 9.5 collective-permute-start.1
  231.8 9.5 collective-permute-start.1
  279.5 9.5 collective-permute-start.1
  291.5 9.5 collective-permute-start.1
  505.9 9.5 collective-permute-start.1
  517.8 9.5 collective-permute-start.1
  732.2 9.5 collective-permute-start.1
  744.1 9.5 collective-permute-start.1
  958.5 9.5 collective-permute-start.1
  970.4 9.5 collective-permute-start.1
  1184.8 9.5 collective-permute-start.1
  1196.7 9.5 collective-permute-start.1
  1411.1 9.5 collective-permute-start.1
  1423.1 9.5 collective-permute-start.1
  (234 other events, 2207.5 us)
where the time goes:
time: 1650 us; the launch traced here: 1640 us
  waiting for transfers between devices  934 us (57%)
  starting transfers between devices  493 us (30%)
  blocking collectives  104 us (6%)
  matrix products  93.3 us (6%)
    ppermute x256, waiting for transfers between devices, passed_along(): return lax.ppermute(value, axis, pairs)  934 us
    ppermute x256, starting transfers between devices, passed_along(): return lax.ppermute(value, axis, pairs)  493 us
    psum x1, blocking collectives, body(): speech_grad, loss = lax.psum((speech_part_sum, loss_part), 'tm')  53 us
  transfers between devices with their start and end apart: 256, of which 256 were waited for; matrix products, arithmetic and copies ran while one was open for 5% of the time, Pallas kernels for 0%

commit v1 on v0

--- a/solution.py
+++ b/solution.py
@@ -8,12 +8,6 @@
 logit_scale = 10.0
 logit_shift = -8.0
 norm_eps = 1e-06
-
-
-def passed_along(value, axis, steps):
-    count = lax.axis_size(axis)
-    pairs = [(source, (source + steps) % count) for source in range(count)]
-    return lax.ppermute(value, axis, pairs)
 
 
 def pair_tile(speech_rows, rec_start, doc_rows, doc_start, doc_index):
@@ -60,32 +54,14 @@
     speech = (
         pooled * lax.rsqrt(jnp.sum(pooled * pooled, axis=1, keepdims=True) + norm_eps)
     ).astype(jnp.bfloat16)
-    group = lax.axis_index("grp")
-    column = lax.axis_index("tm")
-    group_count = lax.axis_size("grp")
-    column_count = lax.axis_size("tm")
-    loss_zero = jnp.zeros((rec_count,), jnp.float32)
-    speech_zero = jnp.zeros((rec_count, width), jnp.float32)
-    doc_zero = jnp.zeros((doc_dev, width), jnp.float32)
-
-    def advance_docs(turn, state_tuple):
-        blocks, grads, losses, speech_acc = state_tuple
-        source = (group - turn) % group_count
-        loss_rows, speech_part, doc_part = pair_tile(
-            speech, group * rec_count, blocks, (source * column_count + column) * doc_dev, doc_index
-        )
-        blocks = passed_along(blocks, "grp", 1)
-        grads = passed_along(grads + doc_part, "grp", 1)
-        return (blocks, grads, losses + loss_rows, speech_acc + speech_part)
-
-    final_state = lax.fori_loop(
-        0, group_count, advance_docs, (doc_embed, doc_zero, loss_zero, speech_zero)
-    )
-    doc_grad = final_state[1]
-    loss_part = final_state[2]
-    speech_part_sum = final_state[3]
-    speech_grad, loss = lax.psum((speech_part_sum, loss_part), "tm")
-    return (loss, speech_grad, doc_grad)
+    doc_start = (lax.axis_index("grp") * lax.axis_size("tm") + lax.axis_index("tm")) * doc_dev
+    all_speech = lax.all_gather(speech, "grp", axis=0, tiled=True)
+    losses, speech_part, doc_grad = pair_tile(all_speech, 0, doc_embed, doc_start, doc_index)
+    loss_rows = jnp.broadcast_to(losses[:, None], (losses.shape[0], 128))
+    packed = jnp.concatenate([speech_part, loss_rows], axis=1)
+    packed = lax.psum_scatter(packed, "grp", scatter_dimension=0, tiled=True)
+    packed = lax.psum(packed, "tm")
+    return (packed[:, width], packed[:, :width], doc_grad)
 
 
 def solution(mesh):

time: 1650 us -> 1310 us (0.79)
  the two profiles are of different devices: /device:TPU:256 before, /device:TPU:6 now
where the time goes in v1:
time: 1310 us
  waiting for transfers between devices  1030 us (79%)
  blocking collectives  255 us (19%)
  between operations  14.8 us (1%)
    unnamed x2, waiting for transfers between devices  1030 us
    all_gather x1, blocking collectives, body(): all_speech = lax.all_gather(speech, 'grp', axis=0, tiled=True)  160 us
    psum x1, blocking collectives, body(): packed = lax.psum(packed, 'tm')  36.7 us
    psum x1, blocking collectives, body(): numerator, totals = lax.psum((numerator, totals), 'tm')  31.8 us
    pmax x1, blocking collectives, body(): peak_score = lax.pmax(jnp.max(masked, axis=2), 'tm')  26.2 us
  transfers between devices with their start and end apart: 1, of which 1 were waited for; matrix products, arithmetic and copies ran while one was open for 0% of the time, Pallas kernels for 0%

profile of v1, /device:TPU:6, one launch (start us, length us, event | category | flops | bytes accessed | tf_op | source)
XLA Modules:
  0.0 1314.1 jit_solution(18135930437233893555)
XLA Ops:
  7.3 0.9 broadcast_compare_fusion
  8.1 0.7 copy-done
  8.8 1.4 fusion.13
  10.2 26.2 %pmax.7 = f32[4,8]{1,0:T(4,128)S(1)} all-reduce(f32[4,8]{1,0:T(4,128)S(1)} %get-tuple-element.18), channel_id=1, replica_groups=mesh['grp'=128,'tm'=8] {'tm'}, use_global_device_ids=true, to_apply=%region_1.2 | all-reduce | flops 32 | bytes 256 | tf_op jit(solution)/shard_map/pmax | solution.py:46
  36.4 2.5 convolution_convert_fusion
  38.9 2.1 reshape.64
  41.1 0.2 fusion.8
  41.2 2.0 fusion
  43.2 31.8 %all-reduce.1 = (f32[4,8,64]{2,1,0:T(8,128)S(1)}, f32[4,8]{1,0:T(4,128)S(1)}) all-reduce(f32[4,8,64]{2,1,0:T(8,128)S(1)} %bitcast.27, f32[4,8]{1,0:T(4,128)S(1)} %get-tuple-element.16), channel_id=1, replica_groups=mesh['grp'=128,'tm'=8] {'tm'}, use_global_device_ids=true, to_apply=%region_2.3 | all-reduce | flops 2080 | bytes 16640 | tf_op jit(solution)/shard_map/psum | solution.py:52
  75.0 0.2 multiply_reduce_fusion
  75.2 0.1 reshape.58
  75.2 0.1 fusion.12
  75.3 160.5 %all-gather = bf16[128,4,512]{2,1,0:T(4,128)(2,1)S(1)} all-gather(bf16[1,4,512]{2,1,0:T(4,128)(2,1)S(1)} %fusion.12), channel_id=1, replica_groups=mesh['grp'=128,'tm'=8] {'grp'}, dimensions={0}, use_global_device_ids=true | all-gather | bytes 528384 | tf_op jit(solution)/shard_map/all_gather | solution.py:58
  235.8 0.1 reshape.60
  236.0 0.3 fusion.6
  236.2 0.4 convolution_multiply_fusion
  236.6 1.2 pad_maximum_fusion
  237.8 1.3 dynamic-slice
  239.8 0.8 convolution_multiply_fusion.2
  240.6 1027.6 %all-reduce.4.cloned.1.call-done = f32[512,640]{0,1:T(8,128)} async-done(((f32[512,640]{0,1:T(8,128)}), f32[512,640]{0,1:T(8,128)}) %all-reduce.4.cloned.1.call-update) | async-done | bytes 1310736
  1268.2 1.1 constant_dynamic-slice_fusion
  1269.3 36.7 %psum.23 = f32[4,640]{0,1:T(8,128)S(1)} all-reduce(f32[4,640]{0,1:T(8,128)S(1)} %constant_dynamic-slice_fusion), channel_id=1, replica_groups=mesh['grp'=128,'tm'=8] {'tm'}, use_global_device_ids=true, to_apply=%region_8.9 | all-reduce | flops 2560 | bytes 20480 | tf_op jit(solution)/shard_map/psum | solution.py:63
  1306.0 0.5 slice_bitcast_fusion
  1306.6 0.7 copy.13
  (12 shorter events, 0.1 us)
Async XLA Ops:
  7.2 1.6 copy-start
  7.2 1261.0 %all-reduce.4.cloned.1.call-start = ((), (), s32[]{:S(2)}) async-start(), calls=%async_computation | async-start | bytes 2621440
  41.1 194.9 %copy-start.1 = (bf16[16,512]{1,0:T(8,128)(2,1)S(1)}, bf16[16,512]{1,0:T(8,128)(2,1)}, u32[]{:S(2)}) copy-start(bf16[16,512]{1,0:T(8,128)(2,1)} %param.10) | copy-start | bytes 49156
  41.1 194.9 %copy-start.2 = (s32[512]{0:T(512)S(1)}, s32[512]{0:T(512)}, u32[]{:S(2)}) copy-start(s32[512]{0:T(512)} %param.11) | copy-start | bytes 6148
Sparse Core Ops, SparseCore 0:
  238.0 1030.2 all-reduce.3

commit v2 on v1

v2 whole, which is shorter than its diff:
```python
import functools
import math

import jax
import jax.numpy as jnp
from jax import lax
from jax.experimental import pallas as pl
from jax.experimental.pallas import tpu as pltpu
from jax.sharding import PartitionSpec as P

logit_scale = 10.0
logit_shift = -8.0
norm_eps = 1e-06
lowest = -1e30

y_hi = 4
cores = 2
lanes = 128


def each(count, step):
    def run(index, carry):
        step(index)
        return carry

    lax.fori_loop(0, count, run, 0)


def iota(shape, axis):
    return lax.broadcasted_iota(jnp.int32, shape, axis)


def dot(a, b, contract_b=0):
    return lax.dot_general(
        a, b, (((1,), (contract_b,)), ((), ())), preferred_element_type=jnp.float32
    )


def kernel(
    rings,
    columns,
    counts_ref,
    index_ref,
    feat_ref,
    query_ref,
    proj_ref,
    docs_ref,
    loss_ref,
    speech_grad_ref,
    doc_grad_ref,
    feat,
    proj,
    docs,
    part_out,
    part_in,
    speech_in,
    target,
    grad_out,
    grad_in,
    total_out,
    total_in,
    doc_out,
    doc_in,
    load_sem,
    docs_sems,
    part_sems,
    speech_sems,
    grad_sems,
    total_sems,
    doc_sems,
):
    recs, frames, channels = feat_ref.shape
    width = proj_ref.shape[1]
    heads = query_ref.shape[0]
    head_width = width // heads
    doc_dev = docs_ref.shape[0]
    halves = columns // y_hi
    pair = recs // halves
    chunks = width // lanes
    rows = rings * 8
    team = columns * cores

    group = lax.axis_index("grp")
    column = lax.axis_index("tm")
    core = lax.rem(group, cores)
    row_y = lax.rem(lax.div(group, cores), y_hi)
    ring = lax.div(group, cores * y_hi)
    me = column * cores + core
    half = lax.rem(lax.div(column, 2), 2)
    served = lax.div(column, 4) * 2 + lax.rem(column, 2)

    def group_of(z, y, c):
        return (z * y_hi + y) * cores + c

    def column_of(y, part):
        return (lax.div(y, 2) * 2 + part) * 2 + lax.rem(y, 2)

    is_server = served == row_y

    def team_peer(step):
        other = lax.rem(me + step + 1, team)
        return other, (group_of(ring, row_y, lax.rem(other, cores)), lax.div(other, cores))

    def ring_peer(step):
        other = lax.rem(ring + step + 1, rings)
        return other, (group_of(other, row_y, core), column)

    def server_peer(step):
        y, part = lax.div(step, halves), lax.rem(step, halves)
        place = column_of(row_y, part)
        return part, (y == row_y) & (place == column), (group_of(ring, y, core), place)

    def client_peer(step):
        return is_server & (step == column), (group_of(ring, served, core), step)

    def remote(source, target_ref, sems, send, receive, device):
        return pltpu.make_async_remote_copy(
            src_ref=source,
            dst_ref=target_ref,
            send_sem=sems.at[0, send],
            recv_sem=sems.at[1, receive],
            device_id=device,
            device_id_type=pl.DeviceIdType.MESH,
        )

    def arrival(buffer, sems, slot):
        pltpu.make_async_copy(buffer.at[slot], buffer.at[slot], sems.at[1, slot]).wait()

    loads = [
        pltpu.make_async_copy(feat_ref.at[rec], feat.at[rec], load_sem.at[rec])
        for rec in range(recs)
    ]
    loads.append(pltpu.make_async_copy(proj_ref, proj, load_sem.at[recs]))
    for load in loads:
        load.start()

    barrier = pltpu.get_barrier_semaphore()

    def greet(device):
        pl.semaphore_signal(
            barrier, inc=1, device_id=device, device_id_type=pl.DeviceIdType.MESH
        )

    each(team - 1, lambda step: greet(team_peer(step)[1]))
    each(rings - 1, lambda step: greet(ring_peer(step)[1]))

    def greet_server(step):
        _, own, device = server_peer(step)

        @pl.when(jnp.logical_not(own))
        def _():
            greet(device)

    def greet_client(step):
        own, device = client_peer(step)

        @pl.when(jnp.logical_not(own))
        def _():
            greet(device)

    each(y_hi * halves, greet_server)
    each(columns, greet_client)

    first_rec = group_of(0, served, core) * recs + half * pair
    odd = (iota((8, lanes), 0) & 1) == 1

    def fill_target(z):
        at = first_rec + z * (y_hi * cores * recs)
        target[pl.ds(pl.multiple_of(z * 8, 8), 8), :] = jnp.where(
            odd, index_ref[at + 1], index_ref[at]
        )

    each(rings, fill_target)
    docs[me] = docs_ref[...]

    lane_head = lax.shift_right_logical(iota((heads, width), 1), int(math.log2(head_width)))
    own_head = lane_head == iota((heads, width), 0)
    position = column * frames + iota((heads, frames), 1)

    def pool(rec):
        loads[rec].wait()
        block = feat[rec]
        scores = dot(query_ref[...], block, 1) / math.sqrt(channels)
        valid = position < counts_ref[rec]
        masked = jnp.where(valid, scores, lowest)
        peak = jnp.max(masked, axis=1, keepdims=True)
        weights = jnp.where(valid, jnp.exp(masked - peak), 0.0)
        total = jnp.sum(weights, axis=1, keepdims=True)
        some = total > 0.0
        safe = jnp.where(some, total, 1.0)
        mean = dot(weights.astype(jnp.bfloat16), block) / safe
        return mean, jnp.where(some, peak + jnp.log(safe), lowest)

    pooled = [pool(0)]

    expected = team - 1 + rings - 1 + y_hi * halves + columns
    pl.semaphore_wait(barrier, expected - jnp.where(is_server, 2, 0))

    def docs_copy(step):
        other, device = team_peer(step)
        return remote(docs.at[me], docs.at[me], docs_sems, other, me, device)

    each(team - 1, lambda step: docs_copy(step).start())

    for rec in range(1, recs):
        pooled.append(pool(rec))
    means = jnp.concatenate([mean for mean, _ in pooled], axis=0)
    high = means.astype(jnp.bfloat16)
    low = (means - high.astype(jnp.float32)).astype(jnp.bfloat16)
    loads[recs].wait()
    projected = dot(jnp.concatenate([high, low], axis=0), proj[...])
    projected = projected[: recs * heads] + projected[recs * heads :]
    for rec in range(recs):
        own = projected[rec * heads : (rec + 1) * heads]
        row = jnp.sum(jnp.where(own_head, own, 0.0), axis=0, keepdims=True)
        level = jnp.sum(jnp.where(own_head, pooled[rec][1], 0.0), axis=0, keepdims=True)
        part, place = rec // pair, rec % pair
        for chunk in range(chunks):
            at = chunk * pair + place
            span = slice(chunk * lanes, (chunk + 1) * lanes)
            part_out[part, at : at + 1, :] = row[:, span]
            part_out[part, 8 + at : 9 + at, :] = level[:, span]

    def part_copy(step):
        part, own, device = server_peer(step)
        return own, part, remote(
            part_out.at[part], part_in.at[column], part_sems, step, column, device
        )

    def part_start(step):
        own, part, copy = part_copy(step)

        @pl.when(jnp.logical_not(own))
        def _():
            copy.start()

        @pl.when(own)
        def _():
            pltpu.make_async_copy(
                part_out.at[part], part_in.at[column], part_sems.at[1, column]
            ).start()

    each(y_hi * halves, part_start)
    each(columns, lambda slot: arrival(part_in, part_sems, slot))

    parts = part_in[...]
    levels = parts[:, 8:, :]
    shares = jnp.exp(levels - jnp.max(levels, axis=0, keepdims=True))
    mean = jnp.sum(shares * parts[:, :8, :], axis=0) / jnp.sum(shares, axis=0)
    squares = mean * mean
    scale_even = lax.rsqrt(jnp.sum(jnp.where(odd, 0.0, squares), keepdims=True) + norm_eps)
    scale_odd = lax.rsqrt(jnp.sum(jnp.where(odd, squares, 0.0), keepdims=True) + norm_eps)
    speech_in[ring] = (mean * jnp.where(odd, scale_odd, scale_even)).astype(jnp.bfloat16)

    def speech_copy(step):
        other, device = ring_peer(step)
        return remote(
            speech_in.at[ring], speech_in.at[ring], speech_sems, other, ring, device
        )

    each(rings - 1, lambda step: speech_copy(step).start())

    def from_others(count, own, buffer, sems):
        each(count - 1, lambda step: arrival(buffer, sems, lax.rem(own + step + 1, count)))

    from_others(team, me, docs, docs_sems)
    from_others(rings, ring, speech_in, speech_sems)

    pieces = speech_in[...].astype(jnp.float32).reshape(rows, lanes).astype(jnp.bfloat16)
    row_at, col_at = iota((rows, rows), 0), iota((rows, rows), 1)
    whole = []
    for chunk in range(chunks):
        pick = col_at == (row_at & -8) + chunk * pair + (row_at & 1)
        pick = jnp.where(pick, 1.0, 0.0).astype(jnp.bfloat16)
        whole.append(dot(pick, pieces).astype(jnp.bfloat16))
    speech = jnp.concatenate(whole, axis=1)
    all_docs = docs[...].reshape(team * doc_dev, width)
    logits = logit_scale * dot(speech, all_docs, 1) + logit_shift

    lane = iota((1, team * doc_dev), 1)
    slot = lax.div(lane, doc_dev)
    doc_group = group_of(ring, row_y, lax.rem(slot, cores))
    doc_id = (doc_group * columns + lax.div(slot, cores)) * doc_dev + lax.rem(lane, doc_dev)
    hit = target[:, :1] == doc_id
    signed = jnp.where(hit, -logits, logits)
    tail = jnp.exp(-jnp.abs(signed))
    losses = jnp.sum(
        jnp.maximum(signed, 0.0) + jnp.log1p(tail), axis=1, keepdims=True
    )
    chance = jnp.where(signed >= 0.0, 1.0, tail) / (1.0 + tail)
    grad = jnp.where(hit, -chance, chance)
    grad_b = grad.astype(jnp.bfloat16)

    chunk_row = lax.shift_right_logical(iota((rows, lanes), 0) & 7, 1)
    wide = dot(grad_b, all_docs)
    picked = jnp.zeros((rows, lanes), jnp.float32)
    for chunk in range(chunks):
        span = slice(chunk * lanes, (chunk + 1) * lanes)
        picked = jnp.where(chunk_row == chunk, wide[:, span], picked)
    loss_high = losses.astype(jnp.bfloat16).astype(jnp.float32)
    loss_low = losses - loss_high
    loss_rows = jnp.where(chunk_row == 0, loss_high, jnp.where(chunk_row == 1, loss_low, 0.0))
    message = jnp.concatenate(
        [picked.reshape(rings, 8, lanes), loss_rows.reshape(rings, 8, lanes)], axis=1
    )
    grad_out[...] = message.astype(jnp.bfloat16)
    grad_in[ring] = grad_out[ring]

    def grad_copy(step):
        other, device = ring_peer(step)
        return remote(grad_out.at[other], grad_in.at[ring], grad_sems, other, ring, device)

    each(rings - 1, lambda step: grad_copy(step).start())

    first_chunk = lax.shift_right_logical(iota((rows, team * doc_dev), 0) & 7, 1) == 0
    once = jnp.where(first_chunk, grad, 0.0).T.astype(jnp.bfloat16)
    doc_part = dot(once, speech).astype(jnp.bfloat16)
    doc_out[...] = doc_part.reshape(team, doc_dev, width)
    doc_in[me] = doc_out[me]

    def doc_copy(step):
        other, device = team_peer(step)
        return remote(doc_out.at[other], doc_in.at[me], doc_sems, other, me, device)

    each(team - 1, lambda step: doc_copy(step).start())

    from_others(rings, ring, grad_in, grad_sems)
    total_out[...] = jnp.sum(grad_in[...].astype(jnp.float32), axis=0)
    place = row_y * halves + half

    def total_copy(step):
        own, device = client_peer(step)
        return own, remote(total_out, total_in.at[place], total_sems, step, place, device)

    def total_start(step):
        own, copy = total_copy(step)

        @pl.when(jnp.logical_not(own))
        def _():
            copy.start()

        @pl.when(own)
        def _():
            pltpu.make_async_copy(
                total_out, total_in.at[place], total_sems.at[1, place]
            ).start()

    each(columns, total_start)

    from_others(team, me, doc_in, doc_sems)
    doc_grad_ref[...] = jnp.sum(doc_in[...].astype(jnp.float32), axis=0)

    each(y_hi * halves, lambda slot: arrival(total_in, total_sems, slot))
    for part in range(halves):
        total = total_in[part]
        for y in range(1, y_hi):
            total += total_in[y * halves + part]
        for place_in in range(pair):
            rec = part * pair + place_in
            for chunk in range(chunks):
                at = chunk * pair + place_in
                speech_grad_ref[rec : rec + 1, chunk * lanes : (chunk + 1) * lanes] = total[
                    at : at + 1
                ]
            high_at, low_at = 8 + place_in, 8 + pair + place_in
            loss_ref[rec : rec + 1, :] = total[high_at : high_at + 1] + total[low_at : low_at + 1]

    each(team - 1, lambda step: docs_copy(step).wait_send())
    each(rings - 1, lambda step: speech_copy(step).wait_send())
    each(rings - 1, lambda step: grad_copy(step).wait_send())
    each(team - 1, lambda step: doc_copy(step).wait_send())

    def part_end(step):
        own, _, copy = part_copy(step)

        @pl.when(jnp.logical_not(own))
        def _():
            copy.wait_send()

    def total_end(step):
        own, copy = total_copy(step)

        @pl.when(jnp.logical_not(own))
        def _():
            copy.wait_send()

    each(y_hi * halves, part_end)
    each(columns, total_end)


def body(groups, columns, features, frame_counts, pool_query, w_proj, doc_embed, doc_index):
    recs, frames, channels = features.shape
    width = w_proj.shape[1]
    doc_dev = doc_embed.shape[0]
    rings = groups // (y_hi * cores)
    halves = columns // y_hi
    team = columns * cores
    smem = pl.BlockSpec(memory_space=pltpu.SMEM)
    vmem = pl.BlockSpec(memory_space=pltpu.VMEM)
    anywhere = pl.BlockSpec(memory_space=pl.ANY)
    f32, bf16 = jnp.float32, jnp.bfloat16
    sems = pltpu.SemaphoreType.DMA
    loss, speech_grad, doc_grad = pl.pallas_call(
        functools.partial(kernel, rings, columns),
        out_shape=(
            jax.ShapeDtypeStruct((recs, lanes), f32),
            jax.ShapeDtypeStruct((recs, width), f32),
            jax.ShapeDtypeStruct((doc_dev, width), f32),
        ),
        in_specs=[smem, smem, anywhere, vmem, anywhere, vmem],
        out_specs=(vmem, vmem, vmem),
        scratch_shapes=[
            pltpu.VMEM((recs, frames, channels), bf16),
            pltpu.VMEM((channels, width), bf16),
            pltpu.VMEM((team, doc_dev, width), bf16),
            pltpu.VMEM((halves, 16, lanes), f32),
            pltpu.VMEM((columns, 16, lanes), f32),
            pltpu.VMEM((rings, 8, lanes), bf16),
            pltpu.VMEM((rings * 8, lanes), jnp.int32),
            pltpu.VMEM((rings, 16, lanes), bf16),
            pltpu.VMEM((rings, 16, lanes), bf16),
            pltpu.VMEM((16, lanes), f32),
            pltpu.VMEM((y_hi * halves, 16, lanes), f32),
            pltpu.VMEM((team, doc_dev, width), bf16),
            pltpu.VMEM((team, doc_dev, width), bf16),
            sems((recs + 1,)),
            sems((2, team)),
            sems((2, max(columns, y_hi * halves))),
            sems((2, rings)),
            sems((2, rings)),
            sems((2, max(columns, y_hi * halves))),
            sems((2, team)),
        ],
        compiler_params=pltpu.CompilerParams(
            collective_id=0, has_side_effects=True, vmem_limit_bytes=32 * 2**20
        ),
    )(frame_counts, doc_index, features, pool_query, w_proj, doc_embed)
    return (loss[:, 0], logit_scale * speech_grad, logit_scale * doc_grad)


def solution(mesh):
    placed = (P("grp", "tm", None), P("grp"), P(), P(), P(("grp", "tm"), None), P())
    return jax.shard_map(
        functools.partial(body, mesh.shape["grp"], mesh.shape["tm"]),
        mesh=mesh,
        in_specs=placed,
        out_specs=(P("grp"), P("grp", None), P(("grp", "tm"), None)),
        check_vma=False,
    )
```

time: 1310 us -> 64.3 us (0.05)
  waiting for transfers between devices: 1030 us -> 0 us
  blocking collectives: 255 us -> 0 us
  Pallas kernels: 0 us -> 55.8 us
  between operations: 14.8 us -> 0.65 us
    unnamed x2 -> x0, waiting for transfers between devices: 1030 us -> none
    all_gather x1 -> x0, blocking collectives: 160 us -> none  [body(): all_speech = lax.all_gather(speech, 'grp', axis=0, tiled=True)]
    psum x2 -> x0, blocking collectives: 68.5 us -> none  [the longest x1 36.7 us: body(): packed = lax.psum(packed, 'tm')]
    pallas_call x0 -> x1, Pallas kernels: none -> 55.8 us  [body(): pl.pallas_call(functools.partial(kernel, rings, columns), out_shape=(jax....]
    pmax x1 -> x0, blocking collectives: 26.2 us -> none  [body(): peak_score = lax.pmax(jnp.max(masked, axis=2), 'tm')]
  transfers between devices with their start and end apart: 1 -> 0, of which waited for: 1 -> 0; matrix products, arithmetic and copies ran while one was open for 0% -> 0% of each run, Pallas kernels for 0% -> 0%
where the time goes in v2:
time: 64.3 us; the launch traced here: 63.9 us
  Pallas kernels  55.8 us (87%)
  local copies, waits for them, and re-layouts  6.2 us (10%)
  other arithmetic  1.22 us (2%)
  between operations  0.65 us (1%)
    pallas_call x1, Pallas kernels, body(): pl.pallas_call(functools.partial(kernel, rings, columns), out_shape=(jax....  55.8 us
    unnamed x12, local copies, waits for them, and re-layouts  5.58 us

profile of v2, /device:TPU:6, one launch (start us, length us, event | category | flops | bytes accessed | tf_op | source)
XLA Modules:
  0.0 63.9 jit_solution(9047116725735336878)
XLA Ops:
  0.6 0.0 copy-start
  0.6 1.6 %copy-done = bf16[4,256,1024]{2,1,0:T(8,128)(2,1)S(1)} copy-done((bf16[4,256,1024]{2,1,0:T(8,128)(2,1)S(1)}, bf16[4,256,1024]{2,1,0:T(8,128)(2,1)}, u32[]{:S(2)}) %copy-start) | copy-done | bytes 2097176
  2.2 0.0 copy-start.1
  2.2 1.2 %copy-done.1 = bf16[1024,512]{1,0:T(8,128)(2,1)S(1)} copy-done((bf16[1024,512]{1,0:T(8,128)(2,1)S(1)}, bf16[1024,512]{1,0:T(8,128)(2,1)}, u32[]{:S(2)}) %copy-start.1) | copy-done | bytes 1048600
  3.4 0.0 copy-start.2
  3.5 0.7 %copy-done.2 = bf16[8,1024]{1,0:T(8,128)(2,1)S(1)} copy-done((bf16[8,1024]{1,0:T(8,128)(2,1)S(1)}, bf16[8,1024]{1,0:T(8,128)(2,1)}, u32[]{:S(2)}) %copy-start.2) | copy-done | bytes 16408
  4.2 0.0 copy-start.3
  4.2 0.7 %copy-done.3 = bf16[16,512]{1,0:T(8,128)(2,1)S(1)} copy-done((bf16[16,512]{1,0:T(8,128)(2,1)S(1)}, bf16[16,512]{1,0:T(8,128)(2,1)}, u32[]{:S(2)}) %copy-start.3) | copy-done | bytes 16408
  4.9 0.0 copy-start.4
  4.9 0.7 %copy-done.4 = s32[512]{0:T(512)S(1)} copy-done((s32[512]{0:T(512)S(1)}, s32[512]{0:T(512)}, u32[]{:S(2)}) %copy-start.4) | copy-done | bytes 2072
  5.6 0.0 copy-start.5
  5.6 0.7 %copy-done.5 = s32[4]{0:T(128)S(1)} copy-done((s32[4]{0:T(128)S(1)}, s32[4]{0:T(128)}, u32[]{:S(2)}) %copy-start.5) | copy-done | bytes 40
  6.2 55.8 %shard_map.85 = (f32[4,128]{1,0:T(4,128)S(1)}, f32[4,512]{1,0:T(4,128)S(1)}, f32[16,512]{1,0:T(8,128)S(1)}) custom-call(s32[4]{0:T(128)S(1)} %copy-done.5, s32[512]{0:T(512)S(1)} %copy-done.4, bf16[4,256,1024]{2,1,0:T(8,128)(2,1)S(1)} %copy-done, bf16[8,1024]{1,0:T(8,128)(2,1)S(1)} %copy-done.2, bf16[1024,512]{1,0:T(8,128)(2,1)S(1)} %copy-done.1, ...), custom_call_target="tpu_custom_call" | custom-call | tf_op jit(solution)/shard_map/pallas_call | solution.py:403
  62.1 0.6 slice_reduce_fusion
  62.7 0.6 broadcast_multiply_fusion.1
  63.3 0.6 broadcast_multiply_fusion
Async XLA Ops:
  0.6 1.6 %copy-start = (bf16[4,256,1024]{2,1,0:T(8,128)(2,1)S(1)}, bf16[4,256,1024]{2,1,0:T(8,128)(2,1)}, u32[]{:S(2)}) copy-start(bf16[4,256,1024]{2,1,0:T(8,128)(2,1)} %feat_ref.1) | copy-start | bytes 6291460
  2.2 1.2 %copy-start.1 = (bf16[1024,512]{1,0:T(8,128)(2,1)S(1)}, bf16[1024,512]{1,0:T(8,128)(2,1)}, u32[]{:S(2)}) copy-start(bf16[1024,512]{1,0:T(8,128)(2,1)} %proj_ref.1) | copy-start | bytes 3145732
  3.4 0.7 %copy-start.2 = (bf16[8,1024]{1,0:T(8,128)(2,1)S(1)}, bf16[8,1024]{1,0:T(8,128)(2,1)}, u32[]{:S(2)}) copy-start(bf16[8,1024]{1,0:T(8,128)(2,1)} %query_ref.1) | copy-start | bytes 49156
  4.2 0.7 %copy-start.3 = (bf16[16,512]{1,0:T(8,128)(2,1)S(1)}, bf16[16,512]{1,0:T(8,128)(2,1)}, u32[]{:S(2)}) copy-start(bf16[16,512]{1,0:T(8,128)(2,1)} %docs_ref.1) | copy-start | bytes 49156
  4.9 0.7 %copy-start.4 = (s32[512]{0:T(512)S(1)}, s32[512]{0:T(512)}, u32[]{:S(2)}) copy-start(s32[512]{0:T(512)} %index_ref.1) | copy-start | bytes 6148
  5.6 0.7 %copy-start.5 = (s32[4]{0:T(128)S(1)}, s32[4]{0:T(128)}, u32[]{:S(2)}) copy-start(s32[4]{0:T(128)} %counts_ref.1) | copy-start | bytes 52

commit v3 on v1

v3 whole, which is shorter than its diff:
```python
import functools
import math

import jax
import jax.numpy as jnp
from jax import lax
from jax.experimental import pallas as pl
from jax.experimental.pallas import tpu as pltpu
from jax.sharding import PartitionSpec as P

logit_scale = 10.0
logit_shift = -8.0
norm_eps = 1e-06
lowest = -1e30

y_hi = 4
cores = 2
lanes = 128


def each(count, step):
    def run(index, carry):
        step(index)
        return carry

    lax.fori_loop(0, count, run, 0)


def bits(count):
    return count.bit_length() - 1


def iota(shape, axis):
    return lax.broadcasted_iota(jnp.int32, shape, axis)


def dot(a, b, contract_b=0):
    return lax.dot_general(
        a, b, (((1,), (contract_b,)), ((), ())), preferred_element_type=jnp.float32
    )


def kernel(
    rings,
    columns,
    counts_ref,
    index_ref,
    feat_ref,
    query_ref,
    proj_ref,
    docs_ref,
    loss_ref,
    speech_grad_ref,
    doc_grad_ref,
    counts,
    index,
    feat,
    query,
    proj,
    docs,
    part_out,
    part_in,
    speech_in,
    target,
    grad_out,
    grad_in,
    total_out,
    total_in,
    doc_out,
    doc_in,
    load_sem,
    docs_sems,
    part_sems,
    speech_sems,
    grad_sems,
    total_sems,
    doc_sems,
):
    recs, frames, channels = feat_ref.shape
    width = proj_ref.shape[1]
    heads = query_ref.shape[0]
    head_width = width // heads
    doc_dev = docs_ref.shape[0]
    halves = columns // y_hi
    pair = recs // halves
    chunks = width // lanes
    rows = rings * 8
    team = columns * cores
    servers = y_hi * halves

    group = lax.axis_index("grp")
    column = lax.axis_index("tm")
    core = group & 1
    row_y = (group >> 1) & (y_hi - 1)
    ring = group >> bits(cores * y_hi)
    me = column * cores + core
    half = (column >> 1) & 1
    served = (column >> 2) * 2 + (column & 1)

    def group_of(z, y, c):
        return (z * y_hi + y) * cores + c

    def column_of(y, part):
        return ((y >> 1) * 2 + part) * 2 + (y & 1)

    is_server = served == row_y

    def team_peer(step):
        other = me ^ (step + 1)
        return other, (group_of(ring, row_y, other & 1), other >> 1)

    def ring_peer(step):
        off = (step + 1) >> 1
        other = (ring + rings // 2 + jnp.where((step & 1) == 1, -off, off)) & (rings - 1)
        return other, (group_of(other, row_y, core), column)

    def server_peer(step):
        y, part = step >> 1, step & 1
        place = column_of(row_y, part)
        return part, (y == row_y) & (place == column), (group_of(ring, y, core), place)

    def client_peer(step):
        return is_server & (step == column), (group_of(ring, served, core), step)

    def remote(source, target_ref, sems, send, receive, device):
        return pltpu.make_async_remote_copy(
            src_ref=source,
            dst_ref=target_ref,
            send_sem=sems.at[0, send],
            recv_sem=sems.at[1, receive],
            device_id=device,
            device_id_type=pl.DeviceIdType.MESH,
        )

    def arrival(buffer, sems, slot):
        pltpu.make_async_copy(buffer.at[slot], buffer.at[slot], sems.at[1, slot]).wait()

    def from_others(count, own, buffer, sems):
        each(count - 1, lambda step: arrival(buffer, sems, own ^ (step + 1)))

    def docs_copy(step):
        other, device = team_peer(step)
        return remote(docs.at[me], docs.at[me], docs_sems, other, me, device)

    def part_copy(step):
        part, own, device = server_peer(step)
        return own, part, remote(
            part_out.at[part], part_in.at[column], part_sems, step, column, device
        )

    def speech_copy(step):
        other, device = ring_peer(step)
        return remote(
            speech_in.at[ring], speech_in.at[ring], speech_sems, other, ring, device
        )

    def grad_copy(step):
        other, device = ring_peer(step)
        return remote(grad_out.at[other], grad_in.at[ring], grad_sems, other, ring, device)

    def doc_copy(step):
        other, device = team_peer(step)
        return remote(doc_out.at[other], doc_in.at[me], doc_sems, other, me, device)

    place_out = row_y * halves + half

    def total_copy(step):
        own, device = client_peer(step)
        return own, remote(
            total_out, total_in.at[place_out], total_sems, step, place_out, device
        )

    loads = [
        pltpu.make_async_copy(source, buffer, load_sem.at[number])
        for number, (source, buffer) in enumerate(
            [
                (feat_ref, feat),
                (query_ref, query),
                (counts_ref, counts),
                (proj_ref, proj),
                (docs_ref, docs.at[me]),
                (index_ref, index),
            ]
        )
    ]
    barrier = pltpu.get_barrier_semaphore()

    def greet(device):
        pl.semaphore_signal(
            barrier, inc=1, device_id=device, device_id_type=pl.DeviceIdType.MESH
        )

    def greet_server(step):
        _, own, device = server_peer(step)

        @pl.when(jnp.logical_not(own))
        def _():
            greet(device)

    def greet_client(step):
        own, device = client_peer(step)

        @pl.when(jnp.logical_not(own))
        def _():
            greet(device)

    def enter():
        for load in loads:
            load.start()
        each(servers, greet_server)
        each(columns, greet_client)
        each(rings - 1, lambda step: greet(ring_peer(step)[1]))
        each(team - 1, lambda step: greet(team_peer(step)[1]))

    def pool():
        for load in loads[:3]:
            load.wait()
        every = feat[...].reshape(recs * frames, channels)
        all_scores = dot(query[...], every, 1) / math.sqrt(channels)
        position = column * frames + iota((heads, frames), 1)
        lane_head = iota((heads, width), 1) >> bits(head_width)
        own_head = lane_head == iota((heads, width), 0)
        means, levels = [], []
        for rec in range(recs):
            scores = all_scores[:, rec * frames : (rec + 1) * frames]
            valid = position < counts[rec]
            masked = jnp.where(valid, scores, lowest)
            peak = jnp.max(masked, axis=1, keepdims=True)
            weights = jnp.where(valid, jnp.exp(masked - peak), 0.0)
            total = jnp.sum(weights, axis=1, keepdims=True)
            some = total > 0.0
            safe = jnp.where(some, total, 1.0)
            means.append(dot(weights.astype(jnp.bfloat16), feat[rec]) / safe)
            levels.append(jnp.where(some, peak + jnp.log(safe), lowest))
        means = jnp.concatenate(means, axis=0)
        high = means.astype(jnp.bfloat16)
        low = (means - high.astype(jnp.float32)).astype(jnp.bfloat16)
        loads[3].wait()
        projected = dot(jnp.concatenate([high, low], axis=0), proj[...])
        projected = projected[: recs * heads] + projected[recs * heads :]
        for rec in range(recs):
            own = projected[rec * heads : (rec + 1) * heads]
            row = jnp.sum(jnp.where(own_head, own, 0.0), axis=0, keepdims=True)
            level = jnp.sum(jnp.where(own_head, levels[rec], 0.0), axis=0, keepdims=True)
            part, place = rec // pair, rec % pair
            for chunk in range(chunks):
                at = chunk * pair + place
                span = slice(chunk * lanes, (chunk + 1) * lanes)
                part_out[part, at : at + 1, :] = row[:, span]
                part_out[part, 8 + at : 9 + at, :] = level[:, span]

    def meet():
        expected = team - 1 + rings - 1 + servers + columns
        pl.semaphore_wait(barrier, expected - jnp.where(is_server, 2, 0))

    def send_parts():
        def start(step):
            own, part, copy = part_copy(step)

            @pl.when(jnp.logical_not(own))
            def _():
                copy.start()

            @pl.when(own)
            def _():
                pltpu.make_async_copy(
                    part_out.at[part], part_in.at[column], part_sems.at[1, column]
                ).start()

        each(servers, start)

    def send_docs():
        loads[4].wait()
        each(team - 1, lambda step: docs_copy(step).start())
        loads[5].wait()
        first_rec = group_of(0, served, core) * recs + half * pair
        odd = (iota((8, lanes), 0) & 1) == 1

        def fill_target(z):
            at = first_rec + z * (y_hi * cores * recs)
            target[pl.ds(pl.multiple_of(z * 8, 8), 8), :] = jnp.where(
                odd, index[at + 1], index[at]
            )

        each(rings, fill_target)

    def merge_parts():
        each(columns, lambda slot: arrival(part_in, part_sems, slot))
        odd = (iota((8, lanes), 0) & 1) == 1
        parts = part_in[...]
        levels = parts[:, 8:, :]
        shares = jnp.exp(levels - jnp.max(levels, axis=0, keepdims=True))
        mean = jnp.sum(shares * parts[:, :8, :], axis=0) / jnp.sum(shares, axis=0)
        squares = mean * mean
        even_sum = jnp.sum(jnp.where(odd, 0.0, squares), keepdims=True)
        odd_sum = jnp.sum(jnp.where(odd, squares, 0.0), keepdims=True)
        scale = lax.rsqrt(jnp.where(odd, odd_sum, even_sum) + norm_eps)
        speech_in[ring] = (mean * scale).astype(jnp.bfloat16)

    def send_speech():
        each(rings - 1, lambda step: speech_copy(step).start())

    def await_speech():
        from_others(team, me, docs, docs_sems)
        from_others(rings, ring, speech_in, speech_sems)

    def score():
        pieces = speech_in[...].astype(jnp.float32).reshape(rows, lanes).astype(jnp.bfloat16)
        row_at, col_at = iota((rows, rows), 0), iota((rows, rows), 1)
        whole = []
        for chunk in range(chunks):
            pick = col_at == (row_at & -8) + chunk * pair + (row_at & 1)
            pick = jnp.where(pick, 1.0, 0.0).astype(jnp.bfloat16)
            whole.append(dot(pick, pieces).astype(jnp.bfloat16))
        speech = jnp.concatenate(whole, axis=1)
        all_docs = docs[...].reshape(team * doc_dev, width)
        logits = logit_scale * dot(speech, all_docs, 1) + logit_shift

        lane = iota((1, team * doc_dev), 1)
        slot = lane >> bits(doc_dev)
        doc_group = group_of(ring, row_y, slot & 1)
        doc_id = (doc_group * columns + (slot >> 1)) * doc_dev + (lane & (doc_dev - 1))
        hit = target[:, :1] == doc_id
        signed = jnp.where(hit, -logits, logits)
        tail = jnp.exp(-jnp.abs(signed))
        losses = jnp.sum(
            jnp.maximum(signed, 0.0) + jnp.log1p(tail), axis=1, keepdims=True
        )
        chance = jnp.where(signed >= 0.0, 1.0, tail) / (1.0 + tail)
        grad = jnp.where(hit, -chance, chance)
        grad_b = grad.astype(jnp.bfloat16)

        chunk_row = (iota((rows, lanes), 0) & 7) >> 1
        wide = dot(grad_b, all_docs)
        picked = jnp.zeros((rows, lanes), jnp.float32)
        for chunk in range(chunks):
            span = slice(chunk * lanes, (chunk + 1) * lanes)
            picked = jnp.where(chunk_row == chunk, wide[:, span], picked)
        loss_high = losses.astype(jnp.bfloat16).astype(jnp.float32)
        loss_low = losses - loss_high
        loss_rows = jnp.where(chunk_row == 0, loss_high, jnp.where(chunk_row == 1, loss_low, 0.0))
        message = jnp.concatenate(
            [picked.reshape(rings, 8, lanes), loss_rows.reshape(rings, 8, lanes)], axis=1
        )
        grad_out[...] = message.astype(jnp.bfloat16)
        grad_in[ring] = grad_out[ring]
        each(rings - 1, lambda step: grad_copy(step).start())

        first_chunk = (iota((rows, team * doc_dev), 0) & 7) >> 1 == 0
        once = jnp.where(first_chunk, grad, 0.0).T.astype(jnp.bfloat16)
        doc_part = dot(once, speech).astype(jnp.bfloat16)
        doc_out[...] = doc_part.reshape(team, doc_dev, width)
        doc_in[me] = doc_out[me]
        each(team - 1, lambda step: doc_copy(step).start())

    def sum_grads():
        from_others(rings, ring, grad_in, grad_sems)
        total_out[...] = jnp.sum(grad_in[...].astype(jnp.float32), axis=0)

        def start(step):
            own, copy = total_copy(step)

            @pl.when(jnp.logical_not(own))
            def _():
                copy.start()

            @pl.when(own)
            def _():
                pltpu.make_async_copy(
                    total_out, total_in.at[place_out], total_sems.at[1, place_out]
                ).start()

        each(columns, start)

    def sum_docs():
        from_others(team, me, doc_in, doc_sems)
        doc_grad_ref[...] = jnp.sum(doc_in[...].astype(jnp.float32), axis=0)

    def sum_totals():
        each(servers, lambda slot: arrival(total_in, total_sems, slot))
        for part in range(halves):
            total = total_in[part]
            for y in range(1, y_hi):
                total += total_in[y * halves + part]
            for place in range(pair):
                rec = part * pair + place
                for chunk in range(chunks):
                    at = chunk * pair + place
                    span = slice(chunk * lanes, (chunk + 1) * lanes)
                    speech_grad_ref[rec : rec + 1, span] = total[at : at + 1]
                high, low = 8 + place, 8 + pair + place
                loss_ref[rec : rec + 1, :] = total[high : high + 1] + total[low : low + 1]

    def drain():
        def part_end(step):
            own, _, copy = part_copy(step)

            @pl.when(jnp.logical_not(own))
            def _():
                copy.wait_send()

        def total_end(step):
            own, copy = total_copy(step)

            @pl.when(jnp.logical_not(own))
            def _():
                copy.wait_send()

        each(servers, part_end)
        each(team - 1, lambda step: docs_copy(step).wait_send())
        each(rings - 1, lambda step: speech_copy(step).wait_send())
        each(rings - 1, lambda step: grad_copy(step).wait_send())
        each(team - 1, lambda step: doc_copy(step).wait_send())
        each(columns, total_end)

    enter()
    pool()
    meet()
    send_parts()
    send_docs()
    merge_parts()
    send_speech()
    await_speech()
    score()
    sum_grads()
    sum_docs()
    sum_totals()
    drain()


def body(groups, columns, features, frame_counts, pool_query, w_proj, doc_embed, doc_index):
    recs, frames, channels = features.shape
    width = w_proj.shape[1]
    doc_dev = doc_embed.shape[0]
    rings = groups // (y_hi * cores)
    halves = columns // y_hi
    team = columns * cores
    vmem = pl.BlockSpec(memory_space=pltpu.VMEM)
    anywhere = pl.BlockSpec(memory_space=pl.ANY)
    f32, bf16 = jnp.float32, jnp.bfloat16
    sems = pltpu.SemaphoreType.DMA
    loss, speech_grad, doc_grad = pl.pallas_call(
        functools.partial(kernel, rings, columns),
        out_shape=(
            jax.ShapeDtypeStruct((recs, lanes), f32),
            jax.ShapeDtypeStruct((recs, width), f32),
            jax.ShapeDtypeStruct((doc_dev, width), f32),
        ),
        in_specs=[anywhere] * 6,
        out_specs=(vmem, vmem, vmem),
        scratch_shapes=[
            pltpu.SMEM(frame_counts.shape, jnp.int32),
            pltpu.SMEM(doc_index.shape, jnp.int32),
            pltpu.VMEM((recs, frames, channels), bf16),
            pltpu.VMEM(pool_query.shape, bf16),
            pltpu.VMEM((channels, width), bf16),
            pltpu.VMEM((team, doc_dev, width), bf16),
            pltpu.VMEM((halves, 16, lanes), f32),
            pltpu.VMEM((columns, 16, lanes), f32),
            pltpu.VMEM((rings, 8, lanes), bf16),
            pltpu.VMEM((rings * 8, lanes), jnp.int32),
            pltpu.VMEM((rings, 16, lanes), bf16),
            pltpu.VMEM((rings, 16, lanes), bf16),
            pltpu.VMEM((16, lanes), f32),
            pltpu.VMEM((y_hi * halves, 16, lanes), f32),
            pltpu.VMEM((team, doc_dev, width), bf16),
            pltpu.VMEM((team, doc_dev, width), bf16),
            sems((6,)),
            sems((2, team)),
            sems((2, max(columns, y_hi * halves))),
            sems((2, rings)),
            sems((2, rings)),
            sems((2, max(columns, y_hi * halves))),
            sems((2, team)),
        ],
        compiler_params=pltpu.CompilerParams(collective_id=0, has_side_effects=True),
    )(frame_counts, doc_index, features, pool_query, w_proj, doc_embed)
    return (loss[:, 0], logit_scale * speech_grad, logit_scale * doc_grad)


def solution(mesh):
    placed = (P("grp", "tm", None), P("grp"), P(), P(), P(("grp", "tm"), None), P())
    return jax.shard_map(
        functools.partial(body, mesh.shape["grp"], mesh.shape["tm"]),
        mesh=mesh,
        in_specs=placed,
        out_specs=(P("grp"), P("grp", None), P(("grp", "tm"), None)),
        check_vma=False,
    )
```

time: 1310 us -> 56.4 us (0.04)
  waiting for transfers between devices: 1030 us -> 0 us
  blocking collectives: 255 us -> 0 us
  Pallas kernels: 0 us -> 51.5 us
  between operations: 14.8 us -> 0.64 us
    unnamed x2 -> x0, waiting for transfers between devices: 1030 us -> none
    all_gather x1 -> x0, blocking collectives: 160 us -> none  [body(): all_speech = lax.all_gather(speech, 'grp', axis=0, tiled=True)]
    psum x2 -> x0, blocking collectives: 68.5 us -> none  [the longest x1 36.7 us: body(): packed = lax.psum(packed, 'tm')]
    pallas_call x0 -> x1, Pallas kernels: none -> 51.5 us  [body(): pl.pallas_call(functools.partial(kernel, rings, columns), out_shape=(jax....]
    pmax x1 -> x0, blocking collectives: 26.2 us -> none  [body(): peak_score = lax.pmax(jnp.max(masked, axis=2), 'tm')]
  transfers between devices with their start and end apart: 1 -> 0, of which waited for: 1 -> 0; matrix products, arithmetic and copies ran while one was open for 0% -> 0% of each run, Pallas kernels for 0% -> 0%
where the time goes in v3:
time: 56.4 us; the launch traced here: 56.1 us
  Pallas kernels  51.5 us (91%)
  other arithmetic  2.67 us (5%)
  local copies, waits for them, and re-layouts  1.29 us (2%)
  between operations  0.64 us (1%)
    pallas_call x1, Pallas kernels, body(): pl.pallas_call(functools.partial(kernel, rings, columns), out_shape=(jax....  51.5 us
    mul x2, other arithmetic, body(): return (loss[:, 0], logit_scale * speech_grad, logit_scale * doc_grad)  2.67 us
    slice x1, local copies, waits for them, and re-layouts, body(): return (loss[:, 0], logit_scale * speech_grad, logit_scale * doc_grad)  1.29 us

profile of v3, /device:TPU:6, one launch (start us, length us, event | category | flops | bytes accessed | tf_op | source)
XLA Modules:
  0.0 56.1 jit_solution(5611133208496541382)
XLA Ops:
  0.6 51.5 %shard_map.85 = (f32[4,128]{1,0:T(4,128)}, f32[4,512]{1,0:T(4,128)}, f32[16,512]{1,0:T(8,128)}) custom-call(s32[4]{0:T(128)} %counts_ref.1, s32[512]{0:T(512)} %index_ref.1, bf16[4,256,1024]{2,1,0:T(8,128)(2,1)} %feat_ref.1, bf16[8,1024]{1,0:T(8,128)(2,1)} %query_ref.1, bf16[1024,512]{1,0:T(8,128)(2,1)} %proj_ref.1, bf16[16,512]{1,0:T(8,128)(2,1)} %docs_ref.1), custom_call_target="tpu_custom_call" | custom-call | tf_op jit(solution)/shard_map/pallas_call | solution.py:442
  52.2 1.3 %slice_reduce_fusion = f32[4]{0:T(128)} fusion(f32[4,128]{1,0:T(4,128)} %get-tuple-element.6), kind=kLoop, calls=%fused_computation.2 | loop fusion | bytes 32 | tf_op jit(solution)/shard_map/slice | solution.py:478
  53.4 1.3 %broadcast_multiply_fusion.1 = f32[4,512]{1,0:T(4,128)} fusion(f32[4,512]{1,0:T(4,128)} %get-tuple-element.7), kind=kLoop, calls=%fused_computation.1 | loop fusion | flops 2048 | bytes 16384 | tf_op jit(solution)/shard_map/mul | solution.py:478
  54.7 1.4 %broadcast_multiply_fusion = f32[16,512]{1,0:T(8,128)} fusion(f32[16,512]{1,0:T(8,128)} %get-tuple-element.8), kind=kLoop, calls=%fused_computation | loop fusion | flops 8192 | bytes 65536 | tf_op jit(solution)/shard_map/mul | solution.py:478

commit v4 on v1

v4 whole, which is shorter than its diff:
```python
import functools
import math

import jax
import jax.numpy as jnp
from jax import lax
from jax.experimental import pallas as pl
from jax.experimental.pallas import tpu as pltpu
from jax.sharding import PartitionSpec as P

logit_scale = 10.0
logit_shift = -8.0
norm_eps = 1e-06
lowest = -1e30

team = 8
lanes = 128


def each(count, step):
    def run(index, carry):
        step(index)
        return carry

    lax.fori_loop(0, count, run, 0)


def bits(count):
    return count.bit_length() - 1


def iota(shape, axis):
    return lax.broadcasted_iota(jnp.int32, shape, axis)


def dot(a, b, contract_b=0):
    return lax.dot_general(
        a, b, (((1,), (contract_b,)), ((), ())), preferred_element_type=jnp.float32
    )


def selector(hit):
    return jnp.where(hit, 1.0, 0.0).astype(jnp.bfloat16)


def kernel(
    rings,
    columns,
    counts_ref,
    index_ref,
    feat_ref,
    query_ref,
    proj_ref,
    docs_ref,
    loss_ref,
    speech_grad_ref,
    doc_grad_ref,
    counts,
    index,
    feat,
    query,
    proj,
    docs,
    part_out,
    part_in,
    speech_in,
    target,
    grad_out,
    grad_in,
    total_out,
    total_in,
    doc_out,
    doc_in,
    load_sem,
    docs_sems,
    part_sems,
    speech_sems,
    grad_sems,
    total_sems,
    doc_sems,
):
    recs, frames, channels = feat_ref.shape
    width = proj_ref.shape[1]
    heads = query_ref.shape[0]
    head_width = width // heads
    doc_dev = docs_ref.shape[0]
    chunks = width // lanes
    packed = chunks * recs

    group = lax.axis_index("grp")
    column = lax.axis_index("tm")
    ring = group >> bits(team)
    member = group & (team - 1)

    def ring_peer(step):
        off = (step + 1) >> 1
        other = (ring + rings // 2 + jnp.where((step & 1) == 1, -off, off)) & (rings - 1)
        return other, (other * team + member, column)

    def team_peer(step):
        other = member ^ (step + 1)
        return other, (ring * team + other, column)

    def column_peer(step):
        other = column ^ (step + 1)
        return other, (group, other)

    class Exchange:
        def __init__(self, count, own, peer, source, buffer, sems, same):
            self.count, self.own, self.peer = count, own, peer
            self.source, self.buffer, self.sems, self.same = source, buffer, sems, same

        def copy(self, step):
            other, device = self.peer(step)
            return pltpu.make_async_remote_copy(
                src_ref=self.source if self.same else self.source.at[other],
                dst_ref=self.buffer.at[self.own],
                send_sem=self.sems.at[0, other],
                recv_sem=self.sems.at[1, self.own],
                device_id=device,
                device_id_type=pl.DeviceIdType.MESH,
            )

        def send(self):
            each(self.count - 1, lambda step: self.copy(step).start())

        def receive(self):
            def arrival(step):
                block = self.buffer.at[self.own ^ (step + 1)]
                pltpu.make_async_copy(
                    block, block, self.sems.at[1, self.own ^ (step + 1)]
                ).wait()

            each(self.count - 1, arrival)

        def drain(self):
            each(self.count - 1, lambda step: self.copy(step).wait_send())

    along_ring = functools.partial(Exchange, rings, ring, ring_peer)
    in_team = functools.partial(Exchange, team, member, team_peer)
    in_column = functools.partial(Exchange, columns, column, column_peer)
    docs_move = in_team(docs.at[member], docs, docs_sems, True)
    part_move = in_column(part_out, part_in, part_sems, True)
    speech_move = along_ring(speech_in.at[ring], speech_in, speech_sems, True)
    grad_move = along_ring(grad_out, grad_in, grad_sems, False)
    total_move = in_column(total_out, total_in, total_sems, True)
    doc_move = in_team(doc_out, doc_in, doc_sems, False)

    loads = [
        pltpu.make_async_copy(source, buffer, load_sem.at[number])
        for number, (source, buffer) in enumerate(
            [
                (feat_ref, feat),
                (query_ref, query),
                (counts_ref, counts),
                (proj_ref, proj),
                (docs_ref, docs.at[member]),
                (index_ref, index),
            ]
        )
    ]
    barrier = pltpu.get_barrier_semaphore()

    def greet(device):
        pl.semaphore_signal(
            barrier, inc=1, device_id=device, device_id_type=pl.DeviceIdType.MESH
        )

    def enter():
        for load in loads:
            load.start()
        each(rings - 1, lambda step: greet(ring_peer(step)[1]))
        each(team - 1, lambda step: greet(team_peer(step)[1]))
        each(columns - 1, lambda step: greet(column_peer(step)[1]))

    def pool():
        for load in loads[:3]:
            load.wait()
        every = feat[...].reshape(recs * frames, channels)
        all_scores = dot(query[...], every, 1) / math.sqrt(channels)
        position = column * frames + iota((heads, frames), 1)
        lane_head = iota((heads, width), 1) >> bits(head_width)
        own_head = lane_head == iota((heads, width), 0)
        means, levels = [], []
        for rec in range(recs):
            scores = all_scores[:, rec * frames : (rec + 1) * frames]
            valid = position < counts[rec]
            masked = jnp.where(valid, scores, lowest)
            peak = jnp.max(masked, axis=1, keepdims=True)
            weights = jnp.where(valid, jnp.exp(masked - peak), 0.0)
            total = jnp.sum(weights, axis=1, keepdims=True)
            some = total > 0.0
            safe = jnp.where(some, total, 1.0)
            means.append(dot(weights.astype(jnp.bfloat16), feat[rec]) / safe)
            levels.append(jnp.where(some, peak + jnp.log(safe), lowest))
        means = jnp.concatenate(means, axis=0)
        high = means.astype(jnp.bfloat16)
        low = (means - high.astype(jnp.float32)).astype(jnp.bfloat16)
        loads[3].wait()
        projected = dot(jnp.concatenate([high, low], axis=0), proj[...])
        projected = projected[: recs * heads] + projected[recs * heads :]
        for rec in range(recs):
            own = projected[rec * heads : (rec + 1) * heads]
            row = jnp.sum(jnp.where(own_head, own, 0.0), axis=0, keepdims=True)
            level = jnp.sum(jnp.where(own_head, levels[rec], 0.0), axis=0, keepdims=True)
            for chunk in range(chunks):
                at = chunk * recs + rec
                span = slice(chunk * lanes, (chunk + 1) * lanes)
                part_out[at : at + 1, :] = row[:, span]
                part_out[packed + at : packed + at + 1, :] = level[:, span]

    def meet():
        pl.semaphore_wait(barrier, rings - 1 + team - 1 + columns - 1)

    def send_parts():
        part_move.send()
        part_in[column] = part_out[...]

    def send_docs():
        loads[4].wait()
        docs_move.send()
        loads[5].wait()
        row = iota((8, lanes), 0)

        def fill(block):
            value = jnp.zeros((8, lanes), jnp.int32)
            for j in range(8):
                place = block * (8 // recs) + j // recs
                number = (place * team + member) * recs + j % recs
                value = jnp.where(row == j, index[number], value)
            target[pl.ds(pl.multiple_of(block * 8, 8), 8), :] = value

        each(rings * recs // 8, fill)

    def merge_parts():
        part_move.receive()
        parts = part_in[...]
        levels = parts[:, packed:, :]
        shares = jnp.exp(levels - jnp.max(levels, axis=0, keepdims=True))
        mean = jnp.sum(shares * parts[:, :packed, :], axis=0) / jnp.sum(shares, axis=0)
        squares = jnp.sum(mean * mean, axis=1, keepdims=True)
        rec_at = iota((packed, 1), 0) & (recs - 1)
        sums = jnp.zeros((packed, 1), jnp.float32)
        for rec in range(recs):
            mine = rec_at == rec
            sums = jnp.where(
                mine, jnp.sum(jnp.where(mine, squares, 0.0), axis=0, keepdims=True), sums
            )
        speech_in[ring] = (mean * lax.rsqrt(sums + norm_eps)).astype(jnp.bfloat16)
        speech_move.send()

    def score():
        docs_move.receive()
        speech_move.receive()
        pieces = speech_in[...].reshape(rings * packed, lanes)
        shape = (rings * recs, rings * packed)
        row, col = iota(shape, 0), iota(shape, 1)
        base = (row >> bits(recs)) * packed + (row & (recs - 1))
        whole = [
            dot(selector(col == base + chunk * recs), pieces).astype(jnp.bfloat16)
            for chunk in range(chunks)
        ]
        speech = jnp.concatenate(whole, axis=1)
        all_docs = docs[...].reshape(team * doc_dev, width)
        logits = logit_scale * dot(speech, all_docs, 1) + logit_shift
        lane = iota((1, team * doc_dev), 1)
        device = (ring * team + (lane >> bits(doc_dev))) * columns + column
        hit = target[:, :1] == device * doc_dev + (lane & (doc_dev - 1))
        signed = jnp.where(hit, -logits, logits)
        tail = jnp.exp(-jnp.abs(signed))
        losses = jnp.sum(jnp.maximum(signed, 0.0) + jnp.log1p(tail), axis=1, keepdims=True)
        chance = jnp.where(signed >= 0.0, 1.0, tail) / (1.0 + tail)
        grad = jnp.where(hit, -chance, chance)

        shape = (rings * packed, rings * recs)
        row, col = iota(shape, 0), iota(shape, 1)
        spread = selector(col == (row >> bits(packed)) * recs + (row & (recs - 1)))
        wide = dot(dot(spread, grad.astype(jnp.bfloat16)).astype(jnp.bfloat16), all_docs)
        chunk_at = (iota((rings * packed, lanes), 0) & (packed - 1)) >> bits(recs)
        picked = wide[:, :lanes]
        for chunk in range(1, chunks):
            span = slice(chunk * lanes, (chunk + 1) * lanes)
            picked = jnp.where(chunk_at == chunk, wide[:, span], picked)

        shape = (rings * 8, rings * recs)
        row, col = iota(shape, 0), iota(shape, 1)
        spread = selector(col == (row >> 3) * recs + (row & (recs - 1)))
        high = jnp.broadcast_to(losses.astype(jnp.bfloat16), (rings * recs, lanes))
        low = (losses - high.astype(jnp.float32)).astype(jnp.bfloat16)
        is_high = (iota((rings * 8, lanes), 0) & 7) < recs
        loss_rows = jnp.where(is_high, dot(spread, high), dot(spread, low))
        message = jnp.concatenate(
            [picked.reshape(rings, packed, lanes), loss_rows.reshape(rings, 8, lanes)], axis=1
        )
        grad_out[...] = message.astype(jnp.bfloat16)
        grad_move.send()
        grad_in[ring] = grad_out[ring]

        doc_part = dot(grad.T.astype(jnp.bfloat16), speech).astype(jnp.bfloat16)
        doc_out[...] = doc_part.reshape(team, doc_dev, width)
        doc_move.send()
        doc_in[member] = doc_out[member]

    def sum_grads():
        grad_move.receive()
        total = jnp.sum(grad_in[...].astype(jnp.float32), axis=0)
        total_out[...] = total
        total_move.send()
        total_in[column] = total

    def sum_docs():
        doc_move.receive()
        doc_grad_ref[...] = logit_scale * jnp.sum(doc_in[...].astype(jnp.float32), axis=0)

    def sum_totals():
        total_move.receive()
        total = jnp.sum(total_in[...], axis=0)
        for chunk in range(chunks):
            span = slice(chunk * lanes, (chunk + 1) * lanes)
            speech_grad_ref[:, span] = logit_scale * total[chunk * recs : (chunk + 1) * recs]
        loss_ref[...] = total[packed : packed + recs] + total[packed + recs : packed + 2 * recs]

    def drain():
        for move in (
            part_move,
            docs_move,
            speech_move,
            grad_move,
            doc_move,
            total_move,
        ):
            move.drain()

    enter()
    pool()
    meet()
    send_parts()
    send_docs()
    merge_parts()
    score()
    sum_grads()
    sum_docs()
    sum_totals()
    drain()


def finish(loss_ref, speech_grad_ref, doc_grad_ref, loss_out, speech_grad_out, doc_grad_out):
    speech_grad_out[...] = speech_grad_ref[...]
    doc_grad_out[...] = doc_grad_ref[...]
    shape = loss_ref.shape
    own = iota(shape, 0) == iota(shape, 1)
    loss_out[...] = jnp.sum(jnp.where(own, loss_ref[...], 0.0), axis=0)[: shape[0]]


def body(groups, columns, features, frame_counts, pool_query, w_proj, doc_embed, doc_index):
    recs, frames, channels = features.shape
    width = w_proj.shape[1]
    doc_dev = doc_embed.shape[0]
    rings = groups // team
    packed = width // lanes * recs
    vmem = pl.BlockSpec(memory_space=pltpu.VMEM)
    f32, bf16, i32 = jnp.float32, jnp.bfloat16, jnp.int32
    sems = pltpu.SemaphoreType.DMA
    loss, speech_grad, doc_grad = pl.pallas_call(
        functools.partial(kernel, rings, columns),
        out_shape=(
            jax.ShapeDtypeStruct((recs, lanes), f32),
            jax.ShapeDtypeStruct((recs, width), f32),
            jax.ShapeDtypeStruct((doc_dev, width), f32),
        ),
        in_specs=[pl.BlockSpec(memory_space=pltpu.MemorySpace.HBM)] * 6,
        out_specs=(vmem, vmem, vmem),
        scratch_shapes=[
            pltpu.SMEM(frame_counts.shape, i32),
            pltpu.SMEM(doc_index.shape, i32),
            pltpu.VMEM(features.shape, bf16),
            pltpu.VMEM(pool_query.shape, bf16),
            pltpu.VMEM(w_proj.shape, bf16),
            pltpu.VMEM((team, doc_dev, width), bf16),
            pltpu.VMEM((2 * packed, lanes), f32),
            pltpu.VMEM((columns, 2 * packed, lanes), f32),
            pltpu.VMEM((rings, packed, lanes), bf16),
            pltpu.VMEM((rings * recs, lanes), i32),
            pltpu.VMEM((rings, packed + 8, lanes), bf16),
            pltpu.VMEM((rings, packed + 8, lanes), bf16),
            pltpu.VMEM((packed + 8, lanes), f32),
            pltpu.VMEM((columns, packed + 8, lanes), f32),
            pltpu.VMEM((team, doc_dev, width), bf16),
            pltpu.VMEM((team, doc_dev, width), bf16),
            sems((6,)),
            sems((2, team)),
            sems((2, columns)),
            sems((2, rings)),
            sems((2, rings)),
            sems((2, columns)),
            sems((2, team)),
        ],
        compiler_params=pltpu.CompilerParams(
            collective_id=0, has_side_effects=True, vmem_limit_bytes=16 * 2**20
        ),
    )(
        *(
            pltpu.with_memory_space_constraint(array, pltpu.MemorySpace.HBM)
            for array in (frame_counts, doc_index, features, pool_query, w_proj, doc_embed)
        )
    )
    return pl.pallas_call(
        finish,
        out_shape=(
            jax.ShapeDtypeStruct((recs,), f32),
            jax.ShapeDtypeStruct((recs, width), f32),
            jax.ShapeDtypeStruct((doc_dev, width), f32),
        ),
        in_specs=[vmem] * 3,
        out_specs=(vmem, vmem, vmem),
        compiler_params=pltpu.CompilerParams(vmem_limit_bytes=16 * 2**20),
    )(loss, speech_grad, doc_grad)


def solution(mesh):
    placed = (P("grp", "tm", None), P("grp"), P(), P(), P(("grp", "tm"), None), P())
    return jax.shard_map(
        functools.partial(body, mesh.shape["grp"], mesh.shape["tm"]),
        mesh=mesh,
        in_specs=placed,
        out_specs=(P("grp"), P("grp", None), P(("grp", "tm"), None)),
        check_vma=False,
    )
```

time: 1310 us -> 49.1 us (0.04)
  waiting for transfers between devices: 1030 us -> 0 us
  blocking collectives: 255 us -> 0 us
  Pallas kernels: 0 us -> 48.3 us
  between operations: 14.8 us -> 0.64 us
    unnamed x2 -> x0, waiting for transfers between devices: 1030 us -> none
    all_gather x1 -> x0, blocking collectives: 160 us -> none  [body(): all_speech = lax.all_gather(speech, 'grp', axis=0, tiled=True)]
    psum x2 -> x0, blocking collectives: 68.5 us -> none  [the longest x1 36.7 us: body(): packed = lax.psum(packed, 'tm')]
    pallas_call x0 -> x2, Pallas kernels: none -> 48.3 us  [the longest x1 47.7 us: body(): pl.pallas_call(functools.partial(kernel, rings, columns), out_shape=(jax....]
    pmax x1 -> x0, blocking collectives: 26.2 us -> none  [body(): peak_score = lax.pmax(jnp.max(masked, axis=2), 'tm')]
  transfers between devices with their start and end apart: 1 -> 0, of which waited for: 1 -> 0; matrix products, arithmetic and copies ran while one was open for 0% -> 0% of each run, Pallas kernels for 0% -> 0%
where the time goes in v4:
time: 49.1 us; the launch traced here: 48.9 us
  Pallas kernels  48.3 us (98%)
  between operations  0.64 us (1%)
    pallas_call x1, Pallas kernels, body(): pl.pallas_call(functools.partial(kernel, rings, columns), out_shape=(jax....  47.7 us

profile of v4, /device:TPU:6, one launch (start us, length us, event | category | flops | bytes accessed | tf_op | source)
XLA Modules:
  0.0 48.9 jit_solution(4203398993572820600)
XLA Ops:
  0.6 47.7 %shard_map.85 = (f32[4,128]{1,0:T(4,128)S(1)}, f32[4,512]{1,0:T(4,128)S(1)}, f32[16,512]{1,0:T(8,128)S(1)}) custom-call(s32[4]{0:T(128)} %counts_ref.1, s32[512]{0:T(512)} %index_ref.1, bf16[4,256,1024]{2,1,0:T(8,128)(2,1)} %feat_ref.1, bf16[8,1024]{1,0:T(8,128)(2,1)} %query_ref.1, bf16[1024,512]{1,0:T(8,128)(2,1)} %proj_ref.1, bf16[16,512]{1,0:T(8,128)(2,1)} %docs_ref.1), custom_call_target="tpu_custom_call" | custom-call | tf_op jit(solution)/shard_map/pallas_call | solution.py:364
  48.3 0.6 %shard_map.86 = (f32[4]{0:T(128)}, f32[4,512]{1,0:T(4,128)}, f32[16,512]{1,0:T(8,128)}) custom-call(f32[4,128]{1,0:T(4,128)S(1)} %get-tuple-element.6.loss_ref, f32[4,512]{1,0:T(4,128)S(1)} %get-tuple-element.7.speech_grad_ref, f32[16,512]{1,0:T(8,128)S(1)} %get-tuple-element.8.doc_grad_ref), custom_call_target="tpu_custom_call" | custom-call | tf_op jit(solution)/shard_map/pallas_call | solution.py:407

commit v5 on v4

--- a/solution.py
+++ b/solution.py
@@ -78,6 +78,8 @@
     grad_sems,
     total_sems,
     doc_sems,
+    column_sem,
+    ring_sem,
 ):
     recs, frames, channels = feat_ref.shape
     width = proj_ref.shape[1]
@@ -169,9 +171,16 @@
     def enter():
         for load in loads:
             load.start()
-        each(rings - 1, lambda step: greet(ring_peer(step)[1]))
-        each(team - 1, lambda step: greet(team_peer(step)[1]))
-        each(columns - 1, lambda step: greet(column_peer(step)[1]))
+        even = column - (column & 1)
+        each(rings - 1, lambda step: greet((ring_peer(step)[1][0], even)))
+        each(team - 1, lambda step: greet((team_peer(step)[1][0], even)))
+
+        def greet_odd(step):
+            @pl.when(step * 2 + 1 != column)
+            def _():
+                greet((group, step * 2 + 1))
+
+        each(columns // 2, greet_odd)
 
     def pool():
         for load in loads[:3]:
@@ -209,8 +218,33 @@
                 part_out[at : at + 1, :] = row[:, span]
                 part_out[packed + at : packed + at + 1, :] = level[:, span]
 
-    def meet():
-        pl.semaphore_wait(barrier, rings - 1 + team - 1 + columns - 1)
+    is_odd = (column & 1) == 1
+
+    def tell_partner(sem):
+        pl.semaphore_signal(
+            sem, inc=1, device_id=(group, column ^ 1), device_id_type=pl.DeviceIdType.MESH
+        )
+
+    def meet_column():
+        @pl.when(is_odd)
+        def _():
+            pl.semaphore_wait(barrier, columns - 1)
+            tell_partner(column_sem)
+
+        @pl.when(jnp.logical_not(is_odd))
+        def _():
+            pl.semaphore_wait(column_sem, 1)
+
+    def open_ring():
+        @pl.when(jnp.logical_not(is_odd))
+        def _():
+            pl.semaphore_wait(barrier, 2 * (rings - 1 + team - 1))
+            tell_partner(ring_sem)
+
+    def meet_ring():
+        @pl.when(is_odd)
+        def _():
+            pl.semaphore_wait(ring_sem, 1)
 
     def send_parts():
         part_move.send()
@@ -219,6 +253,8 @@
     def send_docs():
         loads[4].wait()
         docs_move.send()
+
+    def fill_targets():
         loads[5].wait()
         row = iota((8, lanes), 0)
 
@@ -247,7 +283,6 @@
                 mine, jnp.sum(jnp.where(mine, squares, 0.0), axis=0, keepdims=True), sums
             )
         speech_in[ring] = (mean * lax.rsqrt(sums + norm_eps)).astype(jnp.bfloat16)
-        speech_move.send()
 
     def score():
         docs_move.receive()
@@ -333,10 +368,14 @@
 
     enter()
     pool()
-    meet()
+    meet_column()
     send_parts()
+    fill_targets()
+    open_ring()
+    merge_parts()
+    meet_ring()
+    speech_move.send()
     send_docs()
-    merge_parts()
     score()
     sum_grads()
     sum_docs()
@@ -394,6 +433,8 @@
             sems((2, rings)),
             sems((2, columns)),
             sems((2, team)),
+            pltpu.SemaphoreType.REGULAR,
+            pltpu.SemaphoreType.REGULAR,
         ],
         compiler_params=pltpu.CompilerParams(
             collective_id=0, has_side_effects=True, vmem_limit_bytes=16 * 2**20

time: 49.1 us -> 47.6 us (0.969)
  the two profiles are of different devices: /device:TPU:6 before, /device:TPU:1 now
where the time goes in v5:
time: 47.6 us; the launch traced here: 47.4 us
  Pallas kernels  46.8 us (98%)
  between operations  0.64 us (1%)
    pallas_call x1, Pallas kernels, body(): pl.pallas_call(functools.partial(kernel, rings, columns), out_shape=(jax....  46.1 us

profile of v5, /device:TPU:1, one launch (start us, length us, event | category | flops | bytes accessed | tf_op | source)
XLA Modules:
  0.0 47.4 jit_solution(16016265465717545358)
XLA Ops:
  0.6 46.1 %shard_map.85 = (f32[4,128]{1,0:T(4,128)S(1)}, f32[4,512]{1,0:T(4,128)S(1)}, f32[16,512]{1,0:T(8,128)S(1)}) custom-call(s32[4]{0:T(128)} %counts_ref.1, s32[512]{0:T(512)} %index_ref.1, bf16[4,256,1024]{2,1,0:T(8,128)(2,1)} %feat_ref.1, bf16[8,1024]{1,0:T(8,128)(2,1)} %query_ref.1, bf16[1024,512]{1,0:T(8,128)(2,1)} %proj_ref.1, bf16[16,512]{1,0:T(8,128)(2,1)} %docs_ref.1), custom_call_target="tpu_custom_call" | custom-call | tf_op jit(solution)/shard_map/pallas_call | solution.py:403
  46.8 0.6 %shard_map.86 = (f32[4]{0:T(128)}, f32[4,512]{1,0:T(4,128)}, f32[16,512]{1,0:T(8,128)}) custom-call(f32[4,128]{1,0:T(4,128)S(1)} %get-tuple-element.6.loss_ref, f32[4,512]{1,0:T(4,128)S(1)} %get-tuple-element.7.speech_grad_ref, f32[16,512]{1,0:T(8,128)S(1)} %get-tuple-element.8.doc_grad_ref), custom_call_target="tpu_custom_call" | custom-call | tf_op jit(solution)/shard_map/pallas_call | solution.py:448

commit v6 on v5

--- a/solution.py
+++ b/solution.py
@@ -148,19 +148,14 @@
     total_move = in_column(total_out, total_in, total_sems, True)
     doc_move = in_team(doc_out, doc_in, doc_sems, False)
 
+    sources = [(query_ref, query), (counts_ref, counts)]
+    sources += [(feat_ref.at[rec], feat.at[rec]) for rec in range(recs)]
+    sources += [(proj_ref, proj), (docs_ref, docs.at[member]), (index_ref, index)]
     loads = [
         pltpu.make_async_copy(source, buffer, load_sem.at[number])
-        for number, (source, buffer) in enumerate(
-            [
-                (feat_ref, feat),
-                (query_ref, query),
-                (counts_ref, counts),
-                (proj_ref, proj),
-                (docs_ref, docs.at[member]),
-                (index_ref, index),
-            ]
-        )
+        for number, (source, buffer) in enumerate(sources)
     ]
+    proj_load, docs_load, index_load = loads[-3:]
     barrier = pltpu.get_barrier_semaphore()
 
     def greet(device):
@@ -183,7 +178,7 @@
         each(columns // 2, greet_odd)
 
     def pool():
-        for load in loads[:3]:
+        for load in loads[:-3]:
             load.wait()
         every = feat[...].reshape(recs * frames, channels)
         all_scores = dot(query[...], every, 1) / math.sqrt(channels)
@@ -205,7 +200,7 @@
         means = jnp.concatenate(means, axis=0)
         high = means.astype(jnp.bfloat16)
         low = (means - high.astype(jnp.float32)).astype(jnp.bfloat16)
-        loads[3].wait()
+        proj_load.wait()
         projected = dot(jnp.concatenate([high, low], axis=0), proj[...])
         projected = projected[: recs * heads] + projected[recs * heads :]
         for rec in range(recs):
@@ -251,11 +246,11 @@
         part_in[column] = part_out[...]
 
     def send_docs():
-        loads[4].wait()
+        docs_load.wait()
         docs_move.send()
 
     def fill_targets():
-        loads[5].wait()
+        index_load.wait()
         row = iota((8, lanes), 0)
 
         def fill(block):
@@ -426,7 +421,7 @@
             pltpu.VMEM((columns, packed + 8, lanes), f32),
             pltpu.VMEM((team, doc_dev, width), bf16),
             pltpu.VMEM((team, doc_dev, width), bf16),
-            sems((6,)),
+            sems((recs + 5,)),
             sems((2, team)),
             sems((2, columns)),
             sems((2, rings)),

time: 47.6 us -> 47.6 us (level)
  no operation moved by 1% of the time
where the time goes in v6:
time: 47.6 us; the launch traced here: 47.4 us
  Pallas kernels  46.8 us (98%)
  between operations  0.64 us (1%)
    pallas_call x1, Pallas kernels, body(): pl.pallas_call(functools.partial(kernel, rings, columns), out_shape=(jax....  46.1 us

profile of v6, /device:TPU:1, one launch (start us, length us, event | category | flops | bytes accessed | tf_op | source)
XLA Modules:
  0.0 47.4 jit_solution(303141587153182988)
XLA Ops:
  0.6 46.1 %shard_map.85 = (f32[4,128]{1,0:T(4,128)S(1)}, f32[4,512]{1,0:T(4,128)S(1)}, f32[16,512]{1,0:T(8,128)S(1)}) custom-call(s32[4]{0:T(128)} %counts_ref.1, s32[512]{0:T(512)} %index_ref.1, bf16[4,256,1024]{2,1,0:T(8,128)(2,1)} %feat_ref.1, bf16[8,1024]{1,0:T(8,128)(2,1)} %query_ref.1, bf16[1024,512]{1,0:T(8,128)(2,1)} %proj_ref.1, bf16[16,512]{1,0:T(8,128)(2,1)} %docs_ref.1), custom_call_target="tpu_custom_call" | custom-call | tf_op jit(solution)/shard_map/pallas_call | solution.py:398
  46.8 0.6 %shard_map.86 = (f32[4]{0:T(128)}, f32[4,512]{1,0:T(4,128)}, f32[16,512]{1,0:T(8,128)}) custom-call(f32[4,128]{1,0:T(4,128)S(1)} %get-tuple-element.6.loss_ref, f32[4,512]{1,0:T(4,128)S(1)} %get-tuple-element.7.speech_grad_ref, f32[16,512]{1,0:T(8,128)S(1)} %get-tuple-element.8.doc_grad_ref), custom_call_target="tpu_custom_call" | custom-call | tf_op jit(solution)/shard_map/pallas_call | solution.py:443
